TPU v7x, 32 devices: a whole 2x2x4 slice. The times are simulated.
32 devices in a mesh: groups: 2 (over x), seq: 16 (over z, y, core).
Axes of the slice: x: 2, y: 2, z: 4, core: 2. Of those that a mesh axis runs over, the one named last changes fastest.
Arguments:
- signal: bfloat16 [16384, 2048], P(('groups', 'seq')), parts along dimension 0, may hold values from -6 to 6
- gate_input: bfloat16 [16384, 2048], P(('groups', 'seq')), parts along dimension 0, may hold values from -6 to 6
- cotangent: bfloat16 [16384, 2048], P(('groups', 'seq')), parts along dimension 0, may hold values from -6 to 6
- block_factor: bfloat16 [512, 512], replicated, may hold values from -0.25 to 0.25
- cross_factor: bfloat16 [512, 16, 16], P('seq'), may hold values from -1.5 to 1.5
- order_table: int32 [512], replicated, may hold values from 0 to 511, each once
Outputs:
- grad_signal: bfloat16 [16384, 2048], P(('groups', 'seq')), parts along dimension 0
- grad_gate: bfloat16 [16384, 2048], P(('groups', 'seq')), parts along dimension 0
- grad_block: float32 [1024, 512], P('groups'), parts along dimension 0
- grad_cross: float32 [512, 32, 16], P('seq', 'groups'), parts along dimension 1
There are 2 independent parts, one for each index of `groups`. A program takes and returns all parts, laid end to end along the dimension named above; an argument that names none is the same for every part. Nothing has to cross between parts.
Inputs may be any that keep to these rules, and one draw needn't show every extreme that they name: order_table holds every number of 0 to 511 exactly once.
All inputs are finite; a program needn't handle non-finite values.
Results may differ from a plain program's by a relative error of at most 0.0057.
Values may be sent and summed in bfloat16 or wider, within the bound.
A program may use at most 64 MiB of HBM per device.

v0:
```python
import math

import jax
import jax.numpy as jnp
from jax import lax
from jax.sharding import PartitionSpec as P


def per_device(signal, gate_input, cotangent, block_factor, cross_factor, order_table):
    f32 = jnp.float32
    bf16 = jnp.bfloat16
    count = lax.axis_size("seq")
    width = signal.shape[1]
    permuted = jnp.take(signal, order_table, axis=0)
    mixed = jnp.dot(block_factor, permuted, preferred_element_type=f32).astype(bf16)
    gate_grad = (cotangent.astype(f32) * gate_input.astype(f32)).astype(bf16)
    spread_mixed = lax.all_to_all(mixed[None], "seq", split_axis=1, concat_axis=0, tiled=True)
    spread_grad = lax.all_to_all(gate_grad[None], "seq", split_axis=1, concat_axis=0, tiled=True)
    gated = jnp.einsum(
        "cij,jcd->icd", cross_factor, spread_mixed, preferred_element_type=f32
    ).astype(bf16)
    gated_home = lax.all_to_all(gated, "seq", split_axis=0, concat_axis=1, tiled=True)
    grad_cross = jnp.einsum(
        "icd,jcd->cij", spread_grad, spread_mixed, preferred_element_type=f32
    ) / math.sqrt(width)
    back = jnp.einsum("cij,icd->jcd", cross_factor, spread_grad, preferred_element_type=f32).astype(
        bf16
    )
    back_home = lax.all_to_all(back, "seq", split_axis=0, concat_axis=1, tiled=True)
    grad_gate = (cotangent.astype(f32) * gated_home[0].astype(f32)).astype(bf16)
    back_rows = back_home[0]
    partial_block = lax.dot_general(
        back_rows, permuted, (((1,), (1,)), ((), ())), preferred_element_type=f32
    )
    grad_block = lax.psum(partial_block, "seq") / math.sqrt(count * width)
    spread = lax.dot_general(
        block_factor, back_rows, (((0,), (0,)), ((), ())), preferred_element_type=f32
    ).astype(bf16)
    grad_signal = jnp.zeros_like(spread).at[order_table].set(spread)
    return (grad_signal, grad_gate, grad_block, grad_cross)


def solution(mesh):
    in_specs = (
        P(("groups", "seq"), None),
        P(("groups", "seq"), None),
        P(("groups", "seq"), None),
        P(),
        P("seq", None, None),
        P(),
    )
    out_specs = (
        P(("groups", "seq"), None),
        P(("groups", "seq"), None),
        P("groups", None),
        P("seq", "groups", None),
    )
    return jax.shard_map(
        per_device, mesh=mesh, in_specs=in_specs, out_specs=out_specs, check_vma=False
    )
```

profile of v0, /device:TPU:27, one launch (start us, length us, event | category | flops | bytes accessed | tf_op | source)
XLA Modules:
  0.0 405.5 jit_solution(3647754906035799778)
XLA Ops:
  7.2 0.8 compare_and_fusion
  8.8 3.3 gather_fusion
  12.1 3.1 fusion.3
  15.1 7.7 %copy.32 = bf16[1,512,2048]{2,0,1:T(2,128)(2,1)} copy(bf16[1,512,2048]{1,2,0:T(8,128)(2,1)S(1)} %fusion.3) | data formatting | bytes 4194304 | tf_op jit(solution)/shard_map/broadcast_in_dim | solution.py:17
  23.4 13.2 %reduce = bf16[512,2048]{1,0:T(8,128)(2,1)S(1)} reduce(bf16[512,1,2048]{2,1,0:T(2,128)(2,1)} %bitcast.31, bf16[]{:T(256)} %broadcast.9), dimensions={1}, to_apply=%bitcast.20.reduce_sub_computation | reduce | bytes 4194306
  36.6 2.8 reshape.52
  39.3 6.5 %all-to-all-start.2 = ((bf16[16,2,32768]{2,1,0:T(2,128)(2,1)}), bf16[16,2,32768]{2,1,0:T(2,128)(2,1)S(1)}, u32[]{:S(2)}, u32[]{:S(2)}) async-start(bf16[16,2,32768]{2,1,0:T(2,128)(2,1)} %reshape.52), calls=%async_computation.2 | async-start | bytes 4194304 | tf_op jit(solution)/shard_map/all_to_all | solution.py:17
  46.1 43.9 %all-to-all-done.2 = bf16[16,2,32768]{2,1,0:T(2,128)(2,1)S(1)} async-done(((bf16[16,2,32768]{2,1,0:T(2,128)(2,1)}), bf16[16,2,32768]{2,1,0:T(2,128)(2,1)S(1)}, u32[]{:S(2)}, u32[]{:S(2)}) %all-to-all-start.2) | async-done | bytes 2097184 | tf_op jit(solution)/shard_map/all_to_all | solution.py:17
  90.0 6.7 %reshape.53 = bf16[512,1,2048]{2,1,0:T(2,128)(2,1)} reshape(bf16[16,2,32768]{2,1,0:T(2,128)(2,1)S(1)} %all-to-all-done.2) | data formatting | bytes 4194304
  96.7 3.5 copy.40
  100.1 2.4 fusion.5
  102.6 1.2 copy.35
  103.8 54.5 %all_to_all.42 = bf16[16,32,2048]{2,1,0:T(8,128)(2,1)S(1)} all-to-all(bf16[16,32,2048]{2,1,0:T(8,128)(2,1)S(1)} %copy.35), channel_id=1, replica_groups=mesh['groups'=2,'seq'=16] {'seq'}, dimensions={0} | all-to-all | bytes 4194304 | tf_op jit(solution)/shard_map/all_to_all | solution.py:22
  158.3 3.0 fusion.1
  161.2 5.2 %copy.54 = bf16[1,512,2048]{2,0,1:T(2,128)(2,1)} copy(bf16[1,512,2048]{2,1,0:T(8,128)(2,1)S(1)} %get-tuple-element.17) | data formatting | bytes 4194304 | tf_op jit(solution)/shard_map/broadcast_in_dim | solution.py:18
  166.4 13.2 %reduce.1 = bf16[512,2048]{1,0:T(8,128)(2,1)S(1)} reduce(bf16[512,1,2048]{2,1,0:T(2,128)(2,1)} %bitcast.32, bf16[]{:T(256)} %broadcast.9), dimensions={1}, to_apply=%bitcast.29.reduce_sub_computation | reduce | bytes 4194306
  179.6 2.8 reshape.50
  182.4 52.4 %all_to_all.43 = bf16[16,2,32768]{2,1,0:T(2,128)(2,1)S(1)} all-to-all(bf16[16,2,32768]{2,1,0:T(2,128)(2,1)} %reshape.50), channel_id=1, replica_groups=mesh['groups'=2,'seq'=16] {'seq'}, dimensions={0} | all-to-all | bytes 4194304 | tf_op jit(solution)/shard_map/all_to_all | solution.py:18
  234.8 6.7 %reshape.51 = bf16[512,1,2048]{2,1,0:T(2,128)(2,1)} reshape(bf16[16,2,32768]{2,1,0:T(2,128)(2,1)S(1)} %all_to_all.43) | data formatting | bytes 4194304
  241.5 3.5 copy.39
  245.0 2.4 fusion.4
  247.4 1.2 copy.30
  248.6 52.4 %all_to_all.44 = bf16[16,32,2048]{2,1,0:T(8,128)(2,1)S(1)} all-to-all(bf16[16,32,2048]{2,1,0:T(8,128)(2,1)S(1)} %copy.30), channel_id=1, replica_groups=mesh['groups'=2,'seq'=16] {'seq'}, dimensions={0} | all-to-all | bytes 4194304 | tf_op jit(solution)/shard_map/all_to_all | solution.py:29
  300.9 1.4 copy-done.8
  302.3 2.3 fusion.19
  304.7 3.9 fusion.12
  308.6 0.8 copy.38
  309.4 4.2 %fusion.2 = bf16[512,2048]{0,1:T(8,128)(2,1)} fusion(bf16[512,2048]{1,0:T(8,128)(2,1)} %bitcast.40, bf16[512,512]{1,0:T(8,128)(2,1)S(1)} %copy-done.10), kind=kOutput, calls=%fused_computation.10 | convolution fusion | flops 1074790400 | bytes 4718592 | tf_op jit(solution)/shard_map/dot_general | solution.py:36
  313.6 4.1 %copy.31 = bf16[512,2048]{1,0:T(8,128)(2,1)} copy(bf16[512,2048]{0,1:T(8,128)(2,1)} %fusion.2) | data formatting | bytes 4194304 | tf_op jit(solution)/shard_map/convert_element_type | solution.py:38
  317.7 6.2 %scatter_custom_fusion = bf16[512,2048]{1,0:T(8,128)(2,1)} fusion(s32[512]{0:T(512)S(1)} %compare_select_fusion, bf16[512,2048]{1,0:T(8,128)(2,1)} %copy.31, bf16[]{:T(256)} %constant.8.clone.1), kind=kCustom, calls=%fused_computation.22 | custom fusion | bytes 2097664 | tf_op jit(solution)/shard_map/scatter | solution.py:39
  323.9 72.5 %all-reduce.2.cloned.1.call-done = f32[512,512]{1,0:T(8,128)} async-done(((f32[512,512]{1,0:T(8,128)}), f32[512,512]{1,0:T(8,128)}) %all-reduce.2.cloned.1.call-update) | async-done | bytes 1048592 | tf_op jit(solution)/shard_map/psum | solution.py:35
  396.3 2.3 broadcast_multiply_fusion
  (27 shorter events, 1.5 us)
Async XLA Ops:
  7.2 1.6 copy-start
  8.8 3.3 copy-start.10
  39.3 6.6 %copy-start.9 = (bf16[32,16,16]{0,2,1:T(8,128)(2,1)S(1)}, bf16[32,16,16]{0,2,1:T(8,128)(2,1)}, u32[]{:S(2)}) copy-start(bf16[32,16,16]{0,2,1:T(8,128)(2,1)} %param.10) | copy-start | bytes 49156
  39.3 50.6 %all-to-all-start.2 = ((bf16[16,2,32768]{2,1,0:T(2,128)(2,1)}), bf16[16,2,32768]{2,1,0:T(2,128)(2,1)S(1)}, u32[]{:S(2)}, u32[]{:S(2)}) async-start(bf16[16,2,32768]{2,1,0:T(2,128)(2,1)} %reshape.52), calls=%async_computation.2 | async-start | bytes 4194304 | tf_op jit(solution)/shard_map/all_to_all | solution.py:17
  45.8 350.5 %all-reduce.2.cloned.1.call-start = ((), (), s32[]{:S(2)}) async-start(), calls=%async_computation.4 | async-start | bytes 2097152 | tf_op jit(solution)/shard_map/psum | solution.py:35
  100.1 2.4 copy-start.2
  103.8 54.5 %copy-start.5 = (bf16[512,2048]{1,0:T(8,128)(2,1)S(1)}, bf16[512,2048]{1,0:T(8,128)(2,1)}, u32[]{:S(2)}) copy-start(bf16[512,2048]{1,0:T(8,128)(2,1)} %param.8) | copy-start | bytes 6291460
  103.8 54.5 %copy-start.6 = (bf16[512,2048]{1,0:T(8,128)(2,1)S(1)}, bf16[512,2048]{1,0:T(8,128)(2,1)}, u32[]{:S(2)}) copy-start(bf16[512,2048]{1,0:T(8,128)(2,1)} %param.7) | copy-start | bytes 6291460
  245.0 2.4 copy-start.4
  248.6 53.7 %copy-start.7 = (bf16[512,2048]{1,0:T(8,128)(2,1)S(1)}, bf16[512,2048]{1,0:T(8,128)(2,1)}, u32[]{:S(2)}) copy-start(bf16[512,2048]{1,0:T(8,128)(2,1)} %gather_fusion) | copy-start | bytes 6291460
  300.9 1.4 copy-start.8
  302.3 2.4 copy-start.3
  313.6 85.0 %copy-start.1 = (bf16[512,2048]{1,0:T(8,128)(2,1)S(1)}, bf16[512,2048]{1,0:T(8,128)(2,1)}, u32[]{:S(2)}) copy-start(bf16[512,2048]{1,0:T(8,128)(2,1)} %param.6) | copy-start | bytes 6291460
Sparse Core Ops, SparseCore 0:
  304.8 91.5 all-reduce.1
where the time goes:
time: 410 us; the launch traced here: 405 us
  blocking collectives  159 us (39%)
  waiting for transfers between devices  116 us (28%)
  local copies, waits for them, and re-layouts  57.6 us (14%)
  other arithmetic  33.1 us (8%)
  matrix products  18.4 us (4%)
  between operations  14.2 us (3%)
  starting transfers between devices  6.55 us (2%)
    psum x1, waiting for transfers between devices, per_device(): grad_block = lax.psum(partial_block, 'seq') / math.sqrt(count * width)  72.5 us
    all_to_all x1, blocking collectives, per_device(): lax.all_to_all(gated, 'seq', split_axis=0, concat_axis=1, tiled=True)  54.5 us
    all_to_all x1, blocking collectives, per_device(): lax.all_to_all(gate_grad[None], 'seq', split_axis=1, concat_axis=0, tiled...  52.4 us
    all_to_all x1, blocking collectives, per_device(): lax.all_to_all(back, 'seq', split_axis=0, concat_axis=1, tiled=True)  52.4 us
    all_to_all x1, waiting for transfers between devices, per_device(): lax.all_to_all(mixed[None], 'seq', split_axis=1, concat_axis=0, tiled=True)  43.9 us
    unnamed x31, local copies, waits for them, and re-layouts  28.9 us
    unnamed x2, other arithmetic  26.3 us
  transfers between devices with their start and end apart: 2, of which 2 were waited for; matrix products, arithmetic and copies ran while one was open for 5% of the time, Pallas kernels for 0%

commit v1 on v0

--- a/solution.py
+++ b/solution.py
@@ -1,9 +1,253 @@
+import functools
 import math
 
 import jax
 import jax.numpy as jnp
 from jax import lax
+from jax.experimental import pallas as pl
+from jax.experimental.pallas import tpu as pltpu
 from jax.sharding import PartitionSpec as P
+
+LAYER = 4
+
+
+def log2(value):
+    return value.bit_length() - 1
+
+
+def dot(a, b, ca, cb):
+    return lax.dot_general(a, b, (((ca,), (cb,)), ((), ())), preferred_element_type=jnp.float32)
+
+
+def iota(shape, dim):
+    return lax.broadcasted_iota(jnp.int32, shape, dim)
+
+
+def exchange_kernel(
+    n, sig, gate, cot, bf, crs, order,
+    out_sig, out_gate, out_block, out_cross,
+    gg, mx, pm, bk, gt, rg, rm, rb, rt, pt, bp, wf, pb, s1, ls, s2, gb,
+    send, recv, ar_send, ar_recv,
+):
+    f32, bf16 = jnp.float32, jnp.bfloat16
+    me = lax.axis_index("seq")
+    block, width = sig.shape
+    rows = block // n
+    tile = min(512, width)
+    tiles = width // tile
+    nz = n // LAYER
+    lrows, zrows = block // LAYER, block // n
+    zz, qq = lax.div(me, LAYER), lax.rem(me, LAYER)
+
+    def at(index, size=rows):
+        return pl.ds(pl.multiple_of(index * size, size), size)
+
+    def peer(k):
+        return lax.rem(me + k, n)
+
+    def copy(phase, k, src, dst):
+        return pltpu.make_async_remote_copy(
+            src_ref=src.at[at(peer(k))],
+            dst_ref=dst.at[at(me)],
+            send_sem=send.at[phase, k - 1],
+            recv_sem=recv.at[phase, k - 1],
+            device_id={"seq": peer(k)},
+            device_id_type=pl.DeviceIdType.MESH,
+        )
+
+    def each(body):
+        def step(k, carry):
+            body(k)
+            return carry
+        lax.fori_loop(1, n, step, 0)
+
+    def columns(body):
+        def step(t, carry):
+            body(pl.ds(pl.multiple_of(t * tile, tile), tile))
+            return carry
+        lax.fori_loop(0, tiles, step, 0)
+
+    def own(src, dst):
+        dst[at(me), :] = src[at(me), :]
+
+    barrier = pltpu.get_barrier_semaphore()
+    each(lambda k: pl.semaphore_signal(
+        barrier, inc=1, device_id={"seq": peer(k)}, device_id_type=pl.DeviceIdType.MESH))
+    pl.semaphore_wait(barrier, n - 1)
+
+    def multiply(r):
+        gg[r, :] = (cot[r, :].astype(f32) * gate[r, :].astype(f32)).astype(bf16)
+
+    def first(k):
+        multiply(at(peer(k)))
+        copy(0, k, gg, rg).start()
+
+    each(first)
+    multiply(at(me))
+    own(gg, rg)
+
+    pt[...] = jnp.where(iota((block, block), 0) == order[...], 1.0, 0.0).astype(bf16)
+    bp[...] = dot(bf[...], pt[...], 1, 1).astype(bf16)
+
+    def mix(c):
+        mx[:, c] = dot(bp[...], sig[:, c], 1, 0).astype(bf16)
+
+    columns(mix)
+    each(lambda k: copy(1, k, mx, rm).start())
+    own(mx, rm)
+
+    def permute(c):
+        pm[:, c] = dot(pt[...], sig[:, c], 0, 0).astype(bf16)
+
+    columns(permute)
+
+    sr, sn = log2(rows), log2(n)
+    spread = jnp.where(
+        iota((rows, block), 0) == (iota((rows, block), 1) & (rows - 1)), 1.0, 0.0).astype(bf16)
+    wide = dot(crs[...], spread, 1, 0)
+    keep = (iota((n * n, block), 0) & (n - 1)) == (iota((n * n, block), 1) >> sr)
+    picked = jnp.where(keep, wide, 0.0).astype(bf16)
+    rise = jnp.where(
+        (iota((block, n * n), 0) >> sr) == (iota((block, n * n), 1) >> sn), 1.0, 0.0).astype(bf16)
+    tall = dot(rise, picked, 1, 0)
+    same = (iota((block, block), 0) & (rows - 1)) == (iota((block, block), 1) & (rows - 1))
+    wf[...] = jnp.where(same, tall, 0.0).astype(bf16)
+
+    each(lambda k: copy(0, k, gg, rg).wait_recv())
+
+    def backward(c):
+        bk[:, c] = dot(wf[...], rg[:, c], 0, 0).astype(bf16)
+
+    columns(backward)
+    each(lambda k: copy(2, k, bk, rb).start())
+    own(bk, rb)
+
+    each(lambda k: copy(1, k, mx, rm).wait_recv())
+
+    def forward(c):
+        gt[:, c] = dot(wf[...], rm[:, c], 1, 0).astype(bf16)
+
+    columns(forward)
+    each(lambda k: copy(3, k, gt, rt).start())
+    own(gt, rt)
+
+    half = block // 2
+    for h in range(2):
+        pairs = dot(rg[pl.ds(h * half, half), :], rm[...], 1, 1)
+        match = (iota((half, block), 0) & (rows - 1)) == (iota((half, block), 1) & (rows - 1))
+        pairs = jnp.where(match, pairs, 0.0).reshape(half // rows, rows, block)
+        out_cross[pl.ds(h * (n // 2), n // 2), :] = pairs.sum(axis=1) * (1.0 / math.sqrt(width))
+
+    def layer_peer(d):
+        return lax.rem(qq + d, LAYER)
+
+    def z_peer(d):
+        return lax.rem(zz + d, nz)
+
+    def ar_copy(stage, d, src, dst, device):
+        return pltpu.make_async_remote_copy(
+            src_ref=src, dst_ref=dst,
+            send_sem=ar_send.at[stage, d - 1], recv_sem=ar_recv.at[stage, d - 1],
+            device_id={"seq": device}, device_id_type=pl.DeviceIdType.MESH,
+        )
+
+    each(lambda k: copy(2, k, bk, rb).wait_recv())
+    pb[...] = dot(rb[...], pm[...], 1, 1)
+    one = [ar_copy(0, d, pb.at[at(layer_peer(d), lrows)], s1.at[d - 1], zz * LAYER + layer_peer(d))
+           for d in range(1, LAYER)]
+    for c in one:
+        c.start()
+
+    def back_signal(c):
+        out_sig[:, c] = dot(bp[...], rb[:, c], 0, 0).astype(bf16)
+
+    columns(back_signal)
+    for c in one:
+        c.wait_recv()
+    ls[...] = pb[at(qq, lrows), :] + s1[0] + s1[1] + s1[2]
+    two = [ar_copy(1, d, ls.at[at(z_peer(d), zrows)], s2.at[d - 1], z_peer(d) * LAYER + qq)
+           for d in range(1, nz)]
+    for c in two:
+        c.start()
+    for c in two:
+        c.wait_recv()
+    total = ls[at(zz, zrows), :]
+    for d in range(nz - 1):
+        total = total + s2[d]
+    mine = at(qq * nz + zz, zrows)
+    gb[mine, :] = total * (1.0 / math.sqrt(n * width))
+    three = [ar_copy(2, d, gb.at[mine], gb.at[mine], z_peer(d) * LAYER + qq) for d in range(1, nz)]
+    for c in three:
+        c.start()
+    for c in three:
+        c.wait_recv()
+    layer = at(qq, lrows)
+    four = [ar_copy(3, d, gb.at[layer], gb.at[layer], zz * LAYER + layer_peer(d))
+            for d in range(1, LAYER)]
+    for c in four:
+        c.start()
+
+    def finish(r):
+        out_gate[r, :] = (cot[r, :].astype(f32) * rt[r, :].astype(f32)).astype(bf16)
+
+    finish(at(me))
+
+    def last(k):
+        copy(3, k, gt, rt).wait_recv()
+        finish(at(lax.rem(me + n - k, n)))
+
+    each(last)
+    for c in four:
+        c.wait_recv()
+    out_block[...] = gb[...]
+
+    def drain(k):
+        copy(0, k, gg, rg).wait_send()
+        copy(1, k, mx, rm).wait_send()
+        copy(2, k, bk, rb).wait_send()
+        copy(3, k, gt, rt).wait_send()
+
+    each(drain)
+    for c in one + two + three + four:
+        c.wait_send()
+
+
+def fused(signal, gate_input, cotangent, block_factor, cross_factor, order_table):
+    f32, bf16 = jnp.float32, jnp.bfloat16
+    n = lax.axis_size("seq")
+    block, width = signal.shape
+    rows = block // n
+    nz = n // LAYER
+    crs = cross_factor.transpose(1, 2, 0).reshape(n * n, rows)
+    full = pltpu.VMEM((block, width), bf16)
+    square = pltpu.VMEM((block, block), bf16)
+    vmem = pl.BlockSpec(memory_space=pltpu.VMEM)
+    grad_signal, grad_gate, grad_block, pairs = pl.pallas_call(
+        functools.partial(exchange_kernel, n),
+        out_shape=(
+            jax.ShapeDtypeStruct((block, width), bf16),
+            jax.ShapeDtypeStruct((block, width), bf16),
+            jax.ShapeDtypeStruct((block, block), f32),
+            jax.ShapeDtypeStruct((n, block), f32),
+        ),
+        in_specs=[vmem] * 6,
+        out_specs=(vmem,) * 4,
+        scratch_shapes=[full] * 9 + [square] * 3 + [
+            pltpu.VMEM((block, block), f32),
+            pltpu.VMEM((LAYER - 1, block // LAYER, block), f32),
+            pltpu.VMEM((block // LAYER, block), f32),
+            pltpu.VMEM((nz - 1, block // n, block), f32),
+            pltpu.VMEM((block, block), f32),
+            pltpu.SemaphoreType.DMA((4, n - 1)),
+            pltpu.SemaphoreType.DMA((4, n - 1)),
+            pltpu.SemaphoreType.DMA((4, max(LAYER, nz) - 1)),
+            pltpu.SemaphoreType.DMA((4, max(LAYER, nz) - 1)),
+        ],
+        compiler_params=pltpu.CompilerParams(
+            collective_id=0, has_side_effects=True, vmem_limit_bytes=56 << 20),
+    )(signal, gate_input, cotangent, block_factor, crs, order_table.reshape(1, block))
+    grad_cross = pairs.reshape(n, n, rows).transpose(2, 0, 1)
+    return (grad_signal, grad_gate, grad_block, grad_cross)
 
 
 def per_device(signal, gate_input, cotangent, block_factor, cross_factor, order_table):
@@ -55,6 +299,12 @@
         P("groups", None),
         P("seq", "groups", None),
     )
-    return jax.shard_map(
-        per_device, mesh=mesh, in_specs=in_specs, out_specs=out_specs, check_vma=False
-    )
+
+    def body(signal, *rest):
+        n = mesh.shape["seq"]
+        block = signal.shape[0]
+        whole = block % n == 0 and (block // n) % 16 == 0 and n % (2 * LAYER) == 0
+        whole = whole and n & (n - 1) == 0 and block & (block - 1) == 0
+        return (fused if whole else per_device)(signal, *rest)
+
+    return jax.shard_map(body, mesh=mesh, in_specs=in_specs, out_specs=out_specs, check_vma=False)

time: 410 us -> 227 us (0.55); the launches traced: 405 us -> 227 us
  Pallas kernels: 0 us -> 218 us
  blocking collectives: 159 us -> 0 us
  waiting for transfers between devices: 116 us -> 0 us
  local copies, waits for them, and re-layouts: 57.6 us -> 7.75 us
  other arithmetic: 33.1 us -> 0 us
  matrix products: 18.4 us -> 0 us
  between operations: 14.2 us -> 0.64 us
  starting transfers between devices: 6.55 us -> 0 us
    pallas_call x0 -> x1, Pallas kernels: none -> 218 us  [fused(): pl.pallas_call(functools.partial(exchange_kernel, n), out_shape=(jax.Shap...]
    all_to_all x3 -> x0, blocking collectives: 159 us -> none  [the longest x1 54.5 us: per_device(): lax.all_to_all(gated, 'seq', split_axis=0, concat_axis=1, tiled=True)]
    psum x1 -> x0, waiting for transfers between devices: 72.5 us -> none  [per_device(): grad_block = lax.psum(partial_block, 'seq') / math.sqrt(count * width)]
    all_to_all x1 -> x0, waiting for transfers between devices: 43.9 us -> none  [per_device(): lax.all_to_all(mixed[None], 'seq', split_axis=1, concat_axis=0, tiled=True)]
    unnamed x2 -> x0, other arithmetic: 26.3 us -> none
    unnamed x31 -> x7, local copies, waits for them, and re-layouts: 28.9 us -> 6.24 us
    dot_general x6 -> x0, matrix products: 18.4 us -> none  [the longest x1 4.22 us: per_device(): lax.dot_general(block_factor, back_rows, (((0,), (0,)), ((), ())), prefer...]
    broadcast_in_dim x2 -> x0, local copies, waits for them, and re-layouts: 12.9 us -> none  [the longest x1 7.73 us: per_device(): mixed[None]]
  transfers between devices with their start and end apart: 2 -> 0, of which waited for: 2 -> 0; matrix products, arithmetic and copies ran while one was open for 5% -> 0% of each run, Pallas kernels for 0% -> 0%
where the time goes in v1:
time: 227 us
  Pallas kernels  218 us (96%)
  local copies, waits for them, and re-layouts  7.75 us (3%)
    pallas_call x1, Pallas kernels, fused(): pl.pallas_call(functools.partial(exchange_kernel, n), out_shape=(jax.Shap...  218 us
    unnamed x7, local copies, waits for them, and re-layouts  6.24 us

profile of v1, /device:TPU:27, one launch (start us, length us, event | category | flops | bytes accessed | tf_op | source)
XLA Modules:
  0.0 226.6 jit_solution(3774303350453407054)
XLA Ops:
  0.6 218.3 %shard_map.93 = (bf16[512,2048]{1,0:T(8,128)(2,1)}, bf16[512,2048]{1,0:T(8,128)(2,1)}, f32[512,512]{1,0:T(8,128)}, f32[16,512]{1,0:T(8,128)}) custom-call(bf16[512,2048]{1,0:T(8,128)(2,1)} %sig.1, bf16[512,2048]{1,0:T(8,128)(2,1)} %gate.1, bf16[512,2048]{1,0:T(8,128)(2,1)} %cot.1, bf16[512,512]{1,0:T(8,128)(2,1)} %bf.1, bf16[256,32]{1,0:T(8,128)(2,1)} %bitcast.6, ...), custom_call_target="tpu_custom_call" | custom-call | tf_op jit(solution)/shard_map/pallas_call | solution.py:225
  218.9 1.5 reshape.19
  220.4 0.0 copy-start
  220.4 3.3 %copy.13 = bf16[512,2048]{1,0:T(8,128)(2,1)} copy(bf16[512,2048]{1,0:T(8,128)(2,1)} %get-tuple-element.16) | data formatting | bytes 4194304
  223.7 0.0 copy-done
  223.7 0.0 copy-start.1
  223.7 1.3 copy.14
  225.0 0.6 copy-done.1
  225.7 1.0 copy.15
Async XLA Ops:
  220.4 3.3 %copy-start = (bf16[512,2048]{1,0:T(8,128)(2,1)S(1)}, bf16[512,2048]{1,0:T(8,128)(2,1)}, u32[]{:S(2)}) copy-start(bf16[512,2048]{1,0:T(8,128)(2,1)} %get-tuple-element.17) | copy-start | bytes 6291460
  223.7 2.0 copy-start.1

commit v2 on v1

v2 whole, which is shorter than its diff:
```python
import functools
import math

import jax
import jax.numpy as jnp
from jax import lax
from jax.experimental import pallas as pl
from jax.experimental.pallas import tpu as pltpu
from jax.sharding import PartitionSpec as P

LAYER = 4


def log2(value):
    return value.bit_length() - 1


def dot(a, b, ca, cb):
    return lax.dot_general(a, b, (((ca,), (cb,)), ((), ())), preferred_element_type=jnp.float32)


def iota(shape, dim):
    return lax.broadcasted_iota(jnp.int32, shape, dim)


def exchange_kernel(
    n, gate_in, cot_in, sig_in, order_in, bf_in, crs_in,
    out_sig, out_gate, out_block, out_cross,
    gate, cot, sig, order, bf, crs,
    gg, mx, pm, bk, gt, rg, rm, rb, rt, os, pt, bp, wf,
    pb, s1, ls, s2, ms, s3, gb, gc, send, recv, ar_send, ar_recv, local, closing,
):
    f32, bf16 = jnp.float32, jnp.bfloat16
    me = lax.axis_index("seq")
    block, width = sig.shape
    rows = block // n
    half = width // 2
    tile = min(512, half)
    nz = n // LAYER
    lrows, zrows = block // LAYER, block // LAYER // 2
    zz, qq = lax.div(me, LAYER), lax.rem(me, LAYER)
    left, right, whole = (0, half), (half, half), (0, width)

    def at(index, size=rows):
        return pl.ds(pl.multiple_of(index * size, size), size)

    def peer(k):
        return lax.rem(me + k, n)

    def remote(phase, k):
        src, dst, (start, size) = phases[phase]
        return pltpu.make_async_remote_copy(
            src_ref=src.at[at(peer(k)), pl.ds(start, size)],
            dst_ref=dst.at[at(me), pl.ds(start, size)],
            send_sem=send.at[phase, k - 1],
            recv_sem=recv.at[phase, k - 1],
            device_id={"seq": peer(k)},
            device_id_type=pl.DeviceIdType.MESH,
        )

    phases = [(gg, rg, whole), (mx, rm, left), (bk, rb, whole), (mx, rm, right),
              (gt, rt, left), (gt, rt, right)]

    def each(body):
        def step(k, carry):
            body(k)
            return carry
        lax.fori_loop(1, n, step, 0)

    def columns(part, body):
        def step(t, carry):
            body(pl.ds(pl.multiple_of(part[0] + t * tile, tile), tile))
            return carry
        lax.fori_loop(0, part[1] // tile, step, 0)

    def own(src, dst):
        dst[at(me), :] = src[at(me), :]

    def follow(phase):
        def step(k):
            if phase > 1:
                remote(phase - 2, k).wait_send()
            remote(phase, k).start()
        each(step)

    def arrive(phase):
        each(lambda k: remote(phase, k).wait_recv())

    loads = [pltpu.make_async_copy(src, dst, local.at[i])
             for i, (src, dst) in enumerate([(gate_in, gate), (cot_in, cot), (sig_in, sig),
                                             (order_in, order), (bf_in, bf), (crs_in, crs)])]
    for c in loads:
        c.start()
    barrier = pltpu.get_barrier_semaphore()
    each(lambda k: pl.semaphore_signal(
        barrier, inc=1, device_id={"seq": peer(k)}, device_id_type=pl.DeviceIdType.MESH))
    loads[0].wait()
    loads[1].wait()
    pl.semaphore_wait(barrier, n - 1)

    def multiply(r):
        gg[r, :] = (cot[r, :].astype(f32) * gate[r, :].astype(f32)).astype(bf16)

    def first(k):
        multiply(at(peer(k)))
        remote(0, k).start()

    each(first)
    multiply(at(me))
    own(gg, rg)

    for c in loads[2:]:
        c.wait()
    pt[...] = jnp.where(iota((block, block), 0) == order[...], 1.0, 0.0).astype(bf16)
    bp[...] = dot(bf[...], pt[...], 1, 1).astype(bf16)

    def mix(c):
        mx[:, c] = dot(bp[...], sig[:, c], 1, 0).astype(bf16)
        pm[:, c] = dot(pt[...], sig[:, c], 0, 0).astype(bf16)

    columns(whole, mix)
    own(mx, rm)

    sr, sn = log2(rows), log2(n)
    spread = jnp.where(
        iota((rows, block), 0) == (iota((rows, block), 1) & (rows - 1)), 1.0, 0.0)
    keep = (iota((n * n, block), 0) & (n - 1)) == (iota((n * n, block), 1) >> sr)
    picked = jnp.where(keep, dot(crs[...], spread.astype(bf16), 1, 0), 0.0).astype(bf16)
    rise = jnp.where(
        (iota((block, n * n), 0) >> sr) == (iota((block, n * n), 1) >> sn), 1.0, 0.0).astype(bf16)
    same = (iota((block, block), 0) & (rows - 1)) == (iota((block, block), 1) & (rows - 1))
    wf[...] = jnp.where(same, dot(rise, picked, 1, 0), 0.0).astype(bf16)

    follow(1)

    arrive(0)

    def backward(c):
        bk[:, c] = dot(wf[...], rg[:, c], 0, 0).astype(bf16)

    columns(whole, backward)
    own(bk, rb)
    follow(2)

    def forward(c):
        gt[:, c] = dot(wf[...], rm[:, c], 1, 0).astype(bf16)

    arrive(1)
    columns(left, forward)
    follow(3)

    def layer_peer(d):
        return lax.rem(qq + d, LAYER)

    def z_peer(bit):
        size = 1 << bit
        other = zz + size - 2 * size * lax.rem(lax.div(zz, size), 2)
        return other * LAYER + qq

    def ar_copy(stage, d, src, dst, device):
        return pltpu.make_async_remote_copy(
            src_ref=src, dst_ref=dst,
            send_sem=ar_send.at[stage, d - 1], recv_sem=ar_recv.at[stage, d - 1],
            device_id={"seq": device}, device_id_type=pl.DeviceIdType.MESH,
        )

    arrive(2)
    pb[...] = dot(rb[...], pm[...], 1, 1)
    one = [ar_copy(0, d, pb.at[at(layer_peer(d), lrows)], s1.at[d - 1], zz * LAYER + layer_peer(d))
           for d in range(1, LAYER)]
    for c in one:
        c.start()

    def back_signal(c):
        os[:, c] = dot(bp[...], rb[:, c], 0, 0).astype(bf16)

    columns(whole, back_signal)
    store_sig = pltpu.make_async_copy(os, out_sig, local.at[0])
    store_sig.start()
    for c in one:
        c.wait_recv()
    ls[...] = pb[at(qq, lrows), :] + s1[0] + s1[1] + s1[2]
    even = lax.rem(zz, 2)
    two = [ar_copy(1, 1, ls.at[at(1 - even, zrows)], s2, z_peer(0))]
    two[0].start()

    follow(4)

    two[0].wait_recv()
    ms[0] = ls[at(even, zrows), :] + s2[...]

    def swap(bit):
        return ar_copy(1 + bit, 1, ms.at[bit - 1], s3.at[bit - 1], z_peer(bit))

    swaps = [swap(bit) for bit in range(1, log2(nz))]
    swaps[0].start()

    arrive(3)
    columns(right, forward)
    own(gt, rt)
    follow(5)

    for i, c in enumerate(swaps):
        c.wait_recv()
        ms[i + 1] = ms[i] + s3[i]
        if i + 1 < len(swaps):
            swaps[i + 1].start()
    mine = at(qq * 2 + even, zrows)
    gb[mine, :] = ms[len(swaps)] * (1.0 / math.sqrt(n * width))
    after = 1 + log2(nz)
    three = [ar_copy(after, 1, gb.at[mine], gb.at[mine], z_peer(0))]
    three[0].start()

    hb = block // 2
    for h in range(2):
        pairs = dot(rg[pl.ds(h * hb, hb), :], rm[...], 1, 1)
        match = (iota((hb, block), 0) & (rows - 1)) == (iota((hb, block), 1) & (rows - 1))
        pairs = jnp.where(match, pairs, 0.0).reshape(hb // rows, rows, block).sum(axis=1)
        pairs = jnp.broadcast_to(pairs[:, None, :], (n // 2, n, block)).reshape(n * n // 2, block)
        pairs = jnp.where(keep[: n * n // 2], pairs, 0.0)
        narrow = lax.dot_general(
            pairs, spread, (((1,), (1,)), ((), ())),
            precision=lax.Precision.HIGHEST, preferred_element_type=f32)
        gc[pl.ds(h * (n * n // 2), n * n // 2), :] = narrow * (1.0 / math.sqrt(width))
    store_cross = pltpu.make_async_copy(gc, out_cross, local.at[1])
    store_cross.start()
    three[0].wait_recv()
    layer = at(qq, lrows)
    four = [ar_copy(after + 1, d, gb.at[layer], gb.at[layer], zz * LAYER + layer_peer(d))
            for d in range(1, LAYER)]
    for c in four:
        c.start()

    def finish(r, part):
        c = pl.ds(*part)
        rt[r, c] = (cot[r, c].astype(f32) * rt[r, c].astype(f32)).astype(bf16)

    def close(phase):
        part = phases[phase][2]
        finish(at(me), part)
        stored(phase, 0).start()

        def last(k):
            remote(phase, k).wait_recv()
            finish(at(lax.rem(me + n - k, n)), part)
            stored(phase, k).start()

        each(last)

    def stored(phase, k):
        r, c = at(lax.rem(me + n - k, n)), pl.ds(*phases[phase][2])
        return pltpu.make_async_copy(rt.at[r, c], out_gate.at[r, c], closing.at[phase - 4, k])

    close(4)
    for c in four:
        c.wait_recv()
    store_block = pltpu.make_async_copy(gb, out_block, local.at[2])
    store_block.start()
    close(5)

    def drain(k):
        for phase in (4, 5):
            remote(phase, k).wait_send()
            stored(phase, k).wait()

    for phase in (4, 5):
        stored(phase, 0).wait()
    each(drain)
    for c in one + two + swaps + three + four:
        c.wait_send()
    for c in (store_sig, store_cross, store_block):
        c.wait()


def write_kernel(count, *refs):
    copies = [pltpu.make_async_copy(src, dst, refs[-1].at[i])
              for i, (src, dst) in enumerate(zip(refs[:count], refs[count:]))]
    for c in copies:
        c.start()
    for c in copies:
        c.wait()


def write(*arrays):
    free = pl.BlockSpec(memory_space=pl.ANY)
    return pl.pallas_call(
        functools.partial(write_kernel, len(arrays)),
        out_shape=tuple(jax.ShapeDtypeStruct(x.shape, x.dtype) for x in arrays),
        in_specs=[free] * len(arrays),
        out_specs=(free,) * len(arrays),
        scratch_shapes=[pltpu.SemaphoreType.DMA((len(arrays),))],
        compiler_params=pltpu.CompilerParams(vmem_limit_bytes=1 << 20),
    )(*arrays)


def fused(signal, gate_input, cotangent, block_factor, cross_factor, order_table):
    f32, bf16 = jnp.float32, jnp.bfloat16
    n = lax.axis_size("seq")
    block, width = signal.shape
    rows = block // n
    nz = n // LAYER
    crs = cross_factor.transpose(1, 2, 0).reshape(n * n, rows)
    full = pltpu.VMEM((block, width), bf16)
    square = pltpu.VMEM((block, block), bf16)
    free = pl.BlockSpec(memory_space=pl.ANY)
    inputs = (gate_input, cotangent, signal, order_table.reshape(1, block), block_factor, crs)
    steps = 3 + log2(nz)
    results = pl.pallas_call(
        functools.partial(exchange_kernel, n),
        out_shape=(
            jax.ShapeDtypeStruct((block, width), bf16),
            jax.ShapeDtypeStruct((block, width), bf16),
            jax.ShapeDtypeStruct((block, block), f32),
            jax.ShapeDtypeStruct((n * n, rows), f32),
        ),
        in_specs=[pl.BlockSpec(memory_space=pltpu.HBM)] * 6,
        out_specs=(free,) * 4,
        scratch_shapes=[pltpu.VMEM(x.shape, x.dtype) for x in inputs]
        + [full] * 10 + [square] * 3 + [
            pltpu.VMEM((block, block), f32),
            pltpu.VMEM((LAYER - 1, block // LAYER, block), f32),
            pltpu.VMEM((block // LAYER, block), f32),
            pltpu.VMEM((block // LAYER // 2, block), f32),
            pltpu.VMEM((log2(nz), block // LAYER // 2, block), f32),
            pltpu.VMEM((log2(nz) - 1, block // LAYER // 2, block), f32),
            pltpu.VMEM((block, block), f32),
            pltpu.VMEM((n * n, rows), f32),
            pltpu.SemaphoreType.DMA((6, n - 1)),
            pltpu.SemaphoreType.DMA((6, n - 1)),
            pltpu.SemaphoreType.DMA((steps, LAYER - 1)),
            pltpu.SemaphoreType.DMA((steps, LAYER - 1)),
            pltpu.SemaphoreType.DMA((6,)),
            pltpu.SemaphoreType.DMA((2, n)),
        ],
        compiler_params=pltpu.CompilerParams(
            collective_id=0, has_side_effects=True, vmem_limit_bytes=40 << 20),
    )(*(pltpu.with_memory_space_constraint(x, pltpu.HBM) for x in inputs))
    grad_signal, grad_gate, grad_block, pairs = write(*results)
    grad_cross = pairs.reshape(n, n, rows).transpose(2, 0, 1)
    return (grad_signal, grad_gate, grad_block, grad_cross)


def per_device(signal, gate_input, cotangent, block_factor, cross_factor, order_table):
    f32 = jnp.float32
    bf16 = jnp.bfloat16
    count = lax.axis_size("seq")
    width = signal.shape[1]
    permuted = jnp.take(signal, order_table, axis=0)
    mixed = jnp.dot(block_factor, permuted, preferred_element_type=f32).astype(bf16)
    gate_grad = (cotangent.astype(f32) * gate_input.astype(f32)).astype(bf16)
    spread_mixed = lax.all_to_all(mixed[None], "seq", split_axis=1, concat_axis=0, tiled=True)
    spread_grad = lax.all_to_all(gate_grad[None], "seq", split_axis=1, concat_axis=0, tiled=True)
    gated = jnp.einsum(
        "cij,jcd->icd", cross_factor, spread_mixed, preferred_element_type=f32
    ).astype(bf16)
    gated_home = lax.all_to_all(gated, "seq", split_axis=0, concat_axis=1, tiled=True)
    grad_cross = jnp.einsum(
        "icd,jcd->cij", spread_grad, spread_mixed, preferred_element_type=f32
    ) / math.sqrt(width)
    back = jnp.einsum("cij,icd->jcd", cross_factor, spread_grad, preferred_element_type=f32).astype(
        bf16
    )
    back_home = lax.all_to_all(back, "seq", split_axis=0, concat_axis=1, tiled=True)
    grad_gate = (cotangent.astype(f32) * gated_home[0].astype(f32)).astype(bf16)
    back_rows = back_home[0]
    partial_block = lax.dot_general(
        back_rows, permuted, (((1,), (1,)), ((), ())), preferred_element_type=f32
    )
    grad_block = lax.psum(partial_block, "seq") / math.sqrt(count * width)
    spread = lax.dot_general(
        block_factor, back_rows, (((0,), (0,)), ((), ())), preferred_element_type=f32
    ).astype(bf16)
    grad_signal = jnp.zeros_like(spread).at[order_table].set(spread)
    return (grad_signal, grad_gate, grad_block, grad_cross)


def solution(mesh):
    in_specs = (
        P(("groups", "seq"), None),
        P(("groups", "seq"), None),
        P(("groups", "seq"), None),
        P(),
        P("seq", None, None),
        P(),
    )
    out_specs = (
        P(("groups", "seq"), None),
        P(("groups", "seq"), None),
        P("groups", None),
        P("seq", "groups", None),
    )

    def body(signal, *rest):
        n = mesh.shape["seq"]
        block = signal.shape[0]
        whole = block % n == 0 and (block // n) % 16 == 0 and n % (4 * LAYER) == 0
        whole = whole and n & (n - 1) == 0 and block & (block - 1) == 0
        return (fused if whole else per_device)(signal, *rest)

    return jax.shard_map(body, mesh=mesh, in_specs=in_specs, out_specs=out_specs, check_vma=False)
```

time: 227 us -> 206 us (0.907)
  Pallas kernels: 218 us -> 203 us
  local copies, waits for them, and re-layouts: 7.75 us -> 0 us
    pallas_call x1, Pallas kernels: 218 us -> 200 us  [fused(): pl.pallas_call(functools.partial(exchange_kernel, n), out_shape=(jax.Shap...]
    unnamed x7 -> x0, local copies, waits for them, and re-layouts: 6.24 us -> none
    pallas_call x0 -> x1, Pallas kernels: none -> 2.39 us  [write(): pl.pallas_call(functools.partial(write_kernel, len(arrays)), out_shape=tu...]
where the time goes in v2:
time: 206 us; the launch traced here: 203 us
  Pallas kernels  203 us (99%)
    pallas_call x1, Pallas kernels, fused(): pl.pallas_call(functools.partial(exchange_kernel, n), out_shape=(jax.Shap...  200 us

profile of v2, /device:TPU:27, one launch (start us, length us, event | category | flops | bytes accessed | tf_op | source)
XLA Modules:
  0.0 203.5 jit_solution(10060052424971575969)
XLA Ops:
  0.6 200.4 %shard_map.93 = (bf16[512,2048]{1,0:T(8,128)(2,1)S(1)}, bf16[512,2048]{1,0:T(8,128)(2,1)S(1)}, f32[512,512]{1,0:T(8,128)S(1)}, f32[256,32]{1,0:T(8,128)S(1)}) custom-call(bf16[512,2048]{1,0:T(8,128)(2,1)} %gate_in.1, bf16[512,2048]{1,0:T(8,128)(2,1)} %cot_in.1, bf16[512,2048]{1,0:T(8,128)(2,1)} %sig_in.1, s32[1,512]{1,0:T(1,128)} %bitcast.8, ...), custom_call_target="tpu_custom_call" | custom-call | tf_op jit(solution)/shard_map/pallas_call | solution.py:308
  201.1 2.4 %shard_map.94 = (bf16[512,2048]{1,0:T(8,128)(2,1)}, bf16[512,2048]{1,0:T(8,128)(2,1)}, f32[512,512]{1,0:T(8,128)}, f32[256,32]{1,0:T(8,128)}) custom-call(bf16[512,2048]{1,0:T(8,128)(2,1)S(1)} %get-tuple-element.12.refs_0_, bf16[512,2048]{1,0:T(8,128)(2,1)S(1)} %get-tuple-element.13.refs_1_, f32[512,512]{1,0:T(8,128)S(1)} %get-tuple-element.14.refs_2_, ...), custom_call_target="tpu_custom_call" | custom-call | tf_op jit(solution)/shard_map/pallas_call | solution.py:286

commit v3 on v2

--- a/solution.py
+++ b/solution.py
@@ -196,10 +196,6 @@
     swaps[0].start()
 
     arrive(3)
-    columns(right, forward)
-    own(gt, rt)
-    follow(5)
-
     for i, c in enumerate(swaps):
         c.wait_recv()
         ms[i + 1] = ms[i] + s3[i]
@@ -210,6 +206,17 @@
     after = 1 + log2(nz)
     three = [ar_copy(after, 1, gb.at[mine], gb.at[mine], z_peer(0))]
     three[0].start()
+
+    columns(right, forward)
+    own(gt, rt)
+    follow(5)
+
+    three[0].wait_recv()
+    layer = at(qq, lrows)
+    four = [ar_copy(after + 1, d, gb.at[layer], gb.at[layer], zz * LAYER + layer_peer(d))
+            for d in range(1, LAYER)]
+    for c in four:
+        c.start()
 
     hb = block // 2
     for h in range(2):
@@ -224,13 +231,6 @@
         gc[pl.ds(h * (n * n // 2), n * n // 2), :] = narrow * (1.0 / math.sqrt(width))
     store_cross = pltpu.make_async_copy(gc, out_cross, local.at[1])
     store_cross.start()
-    three[0].wait_recv()
-    layer = at(qq, lrows)
-    four = [ar_copy(after + 1, d, gb.at[layer], gb.at[layer], zz * LAYER + layer_peer(d))
-            for d in range(1, LAYER)]
-    for c in four:
-        c.start()
-
     def finish(r, part):
         c = pl.ds(*part)
         rt[r, c] = (cot[r, c].astype(f32) * rt[r, c].astype(f32)).astype(bf16)

time: 206 us -> 201 us (0.976)
  Pallas kernels: 203 us -> 196 us
    pallas_call x1, Pallas kernels: 200 us -> 194 us  [fused(): pl.pallas_call(functools.partial(exchange_kernel, n), out_shape=(jax.Shap...]
where the time goes in v3:
time: 201 us; the launch traced here: 197 us
  Pallas kernels  196 us (98%)
    pallas_call x1, Pallas kernels, fused(): pl.pallas_call(functools.partial(exchange_kernel, n), out_shape=(jax.Shap...  194 us

profile of v3, /device:TPU:27, one launch (start us, length us, event | category | flops | bytes accessed | tf_op | source)
XLA Modules:
  0.0 197.1 jit_solution(9077689803752770738)
XLA Ops:
  0.6 194.1 %shard_map.93 = (bf16[512,2048]{1,0:T(8,128)(2,1)S(1)}, bf16[512,2048]{1,0:T(8,128)(2,1)S(1)}, f32[512,512]{1,0:T(8,128)S(1)}, f32[256,32]{1,0:T(8,128)S(1)}) custom-call(bf16[512,2048]{1,0:T(8,128)(2,1)} %gate_in.1, bf16[512,2048]{1,0:T(8,128)(2,1)} %cot_in.1, bf16[512,2048]{1,0:T(8,128)(2,1)} %sig_in.1, s32[1,512]{1,0:T(1,128)} %bitcast.8, ...), custom_call_target="tpu_custom_call" | custom-call | tf_op jit(solution)/shard_map/pallas_call | solution.py:308
  194.7 2.4 %shard_map.94 = (bf16[512,2048]{1,0:T(8,128)(2,1)}, bf16[512,2048]{1,0:T(8,128)(2,1)}, f32[512,512]{1,0:T(8,128)}, f32[256,32]{1,0:T(8,128)}) custom-call(bf16[512,2048]{1,0:T(8,128)(2,1)S(1)} %get-tuple-element.12.refs_0_, bf16[512,2048]{1,0:T(8,128)(2,1)S(1)} %get-tuple-element.13.refs_1_, f32[512,512]{1,0:T(8,128)S(1)} %get-tuple-element.14.refs_2_, ...), custom_call_target="tpu_custom_call" | custom-call | tf_op jit(solution)/shard_map/pallas_call | solution.py:286
